TPU v7x, 256 devices: a whole 4x4x8 slice. The times are simulated.
256 devices in a mesh: pp: 2 (over x_hi), dp: 8 (over y, core), cp: 16 (over z, x_lo).
Axes of the slice: x: 4 (x_hi: 2, x_lo: 2; x = x_hi * 2 + x_lo), y: 4, z: 8, core: 2. Of those that a mesh axis runs over, the one named last changes fastest.
Arguments:
- tokens: bfloat16 [2, 2048, 3584], P('pp', 'cp'), may hold values from -6 to 6
- out_grad: bfloat16 [2, 2048, 3584], P('pp', 'cp'), may hold values from -6 to 6
- probs: bfloat16 [2, 2048, 8], P('pp', 'cp'), may hold values from 0.019897461 to 0.29882812
- expert_ids: int32 [2, 2048, 8], P('pp', 'cp'), may hold values from 0 to 15, all different within a row; in each aligned block of 128 rows (0 to 127, 128 to 255, ..., all dimensions but the last counted through in order) at most 80 rows name the same one
- w_gate: bfloat16 [2, 16, 1280, 3584], P('pp', 'cp', 'dp'), may hold values from -0.09375 to 0.09375
- w_up: bfloat16 [2, 16, 1280, 3584], P('pp', 'cp', 'dp'), may hold values from -0.09375 to 0.09375
- w_down: bfloat16 [2, 16, 1280, 3584], P('pp', 'cp', 'dp'), may hold values from -0.15625 to 0.15625
Outputs:
- passed_grad: bfloat16 [2, 2048, 3584], P('pp', 'cp', 'dp')
- prob_grad: float32 [2, 2048, 8], P('pp', 'cp')
- gate_grad: bfloat16 [2, 16, 1280, 3584], P('pp', 'cp', 'dp')
- up_grad: bfloat16 [2, 16, 1280, 3584], P('pp', 'cp', 'dp')
- down_grad: bfloat16 [2, 16, 1280, 3584], P('pp', 'cp', 'dp')
Inputs may be any that keep to these rules, and one draw needn't show every extreme that they name: `expert_ids`: in each aligned block of 128 tokens of a section, a token names 8 different experts, and no expert is named by more than 80 tokens of the block; some expert is named by exactly 80 tokens of some block.
All inputs are finite; a program needn't handle non-finite values.
Results may differ from a plain program's by a relative error of at most 0.012.
Values may be sent and summed in bfloat16 or wider, within the bound.
A program may use at most 128 MiB of HBM per device.

v0:
```python
import jax
import jax.numpy as jnp
from jax import lax
from jax.sharding import PartitionSpec as P

CAP_NUM, CAP_DEN = (5, 4)


def body(tokens, out_grad, probs, expert_ids, w_gate, w_up, w_down):
    tok_rows = tokens.shape[1]
    width = tokens.shape[2]
    top_count = probs.shape[2]
    experts = lax.axis_size("cp")
    replicas = lax.axis_size("dp")
    capacity = tok_rows * top_count * CAP_NUM // (CAP_DEN * experts)
    columns = width // replicas
    dp = lax.axis_index("dp")
    me = lax.axis_index("cp")
    own = lax.dynamic_slice_in_dim(jnp.stack([tokens[0], out_grad[0]]), dp * columns, columns, 2)
    blocks = lax.all_gather(own, "cp")
    ids_all = lax.all_gather(expert_ids[0], "cp")
    probs_all = lax.all_gather(probs[0], "cp")
    match = ids_all == me
    has = jnp.any(match, axis=2)
    prob_tok = jnp.sum(jnp.where(match, probs_all.astype(jnp.float32), 0.0), axis=2)
    has_i = has.astype(jnp.int32)
    slot = jnp.cumsum(has_i, axis=1) - has_i
    pick = (slot[:, None, :] == jnp.arange(capacity)[None, :, None]) & has[:, None, :]
    probs_in = jnp.sum(jnp.where(pick, prob_tok[:, None, :], 0.0), axis=2).reshape(-1, 1)
    rows = jnp.einsum(
        "bct,bstd->sbcd", pick.astype(jnp.bfloat16), blocks, preferred_element_type=jnp.float32
    ).astype(jnp.bfloat16)
    total_rows = experts * capacity
    rows = rows.reshape(2 * total_rows, columns)
    full = lax.all_gather(rows, "dp", axis=1, tiled=True)
    rows_in, grads_in = (full[:total_rows], full[total_rows:])
    gate_mat = w_gate[0, 0]
    up_mat = w_up[0, 0]
    down_mat = w_down[0, 0]
    by_feature = (((1,), (1,)), ((), ()))
    by_row = (((0,), (0,)), ((), ()))
    gate_pre = lax.dot_general(rows_in, gate_mat, by_feature, preferred_element_type=jnp.float32)
    up_pre = lax.dot_general(rows_in, up_mat, by_feature, preferred_element_type=jnp.float32)
    grad_proj = lax.dot_general(grads_in, down_mat, by_feature, preferred_element_type=jnp.float32)
    sigma = jax.nn.sigmoid(gate_pre)
    silu_gate = gate_pre * sigma
    hidden = (silu_gate * up_pre).astype(jnp.bfloat16)
    prob_part = jnp.sum(hidden.astype(jnp.float32) * grad_proj, axis=1)
    grad_hidden = probs_in * grad_proj
    grad_gate_pre = (grad_hidden * up_pre * sigma * (1.0 + gate_pre * (1.0 - sigma))).astype(
        jnp.bfloat16
    )
    grad_up_pre = (grad_hidden * silu_gate).astype(jnp.bfloat16)
    scaled_hidden = hidden
    scaled_grad = (probs_in * grads_in).astype(jnp.bfloat16)
    input_part = jnp.dot(grad_gate_pre, gate_mat, preferred_element_type=jnp.float32)
    input_part = (
        input_part + jnp.dot(grad_up_pre, up_mat, preferred_element_type=jnp.float32)
    ).astype(jnp.bfloat16)
    gate_grad = lax.dot_general(
        grad_gate_pre, rows_in, by_row, preferred_element_type=jnp.float32
    ).astype(jnp.bfloat16)
    up_grad = lax.dot_general(
        grad_up_pre, rows_in, by_row, preferred_element_type=jnp.float32
    ).astype(jnp.bfloat16)
    down_grad = lax.dot_general(
        scaled_hidden, scaled_grad, by_row, preferred_element_type=jnp.float32
    ).astype(jnp.bfloat16)
    reduced = lax.psum_scatter(input_part, "dp", scatter_dimension=1, tiled=True)
    back = lax.all_to_all(
        reduced.reshape(experts, capacity, columns), "cp", split_axis=0, concat_axis=0, tiled=True
    )
    back_probs = lax.all_to_all(
        prob_part.reshape(experts, capacity), "cp", split_axis=0, concat_axis=0, tiled=True
    )
    back_probs = lax.psum(back_probs, "dp")
    one_hot = expert_ids[0][:, :, None] == jnp.arange(experts)[None, None, :]
    has_e = jnp.any(one_hot, axis=1).astype(jnp.int32)
    slot_e = jnp.cumsum(has_e, axis=0) - has_e
    pick_e = (slot_e[:, :, None] == jnp.arange(capacity)[None, None, :]) & (has_e[:, :, None] > 0)
    input_sum = jnp.dot(
        pick_e.reshape(tok_rows, total_rows).astype(jnp.bfloat16),
        back.reshape(total_rows, columns),
        preferred_element_type=jnp.float32,
    )
    prob_te = jnp.sum(jnp.where(pick_e, back_probs[None], 0.0), axis=2)
    prob_grad = jnp.sum(jnp.where(one_hot, prob_te[:, None, :], 0.0), axis=2)
    passed = lax.ppermute(input_sum.astype(jnp.bfloat16), "pp", [(1, 0)])
    return (
        passed[None],
        prob_grad[None],
        gate_grad[None, None],
        up_grad[None, None],
        down_grad[None, None],
    )


def solution(mesh):
    in_specs = (
        P("pp", "cp", None),
        P("pp", "cp", None),
        P("pp", "cp", None),
        P("pp", "cp", None),
        P("pp", "cp", "dp", None),
        P("pp", "cp", "dp", None),
        P("pp", "cp", "dp", None),
    )
    out_specs = (
        P("pp", "cp", "dp"),
        P("pp", "cp", None),
        P("pp", "cp", "dp", None),
        P("pp", "cp", "dp", None),
        P("pp", "cp", "dp", None),
    )
    return jax.shard_map(body, mesh=mesh, in_specs=in_specs, out_specs=out_specs, check_vma=False)
```

profile of v0, /device:TPU:2, one launch (start us, length us, event | category | flops | bytes accessed | tf_op | source)
XLA Modules:
  0.0 369.4 jit_solution(6365457031545415939)
XLA Ops:
  7.2 0.0 copy-start
  7.2 0.0 all-gather.6.cloned.1.call-start
  7.3 1.6 copy.35
  8.9 1.6 copy.36
  10.5 0.7 fusion.45
  11.2 0.0 all-gather.6.cloned.1.call-update
  11.2 0.0 all-gather.4.cloned.1.call-start
  11.3 33.8 %all_gather.16 = bf16[16,128,8]{1,2,0:T(8,128)(2,1)S(1)} all-gather(bf16[1,128,8]{1,2,0:T(8,128)(2,1)S(1)} %copy-done.4), channel_id=1, replica_groups=mesh['pp'=2,'dp'=8,'cp'=16] {'cp'}, dimensions={0}, use_global_device_ids=true | all-gather | bytes 34816 | tf_op jit(solution)/shard_map/all_gather | solution.py:22
  45.1 33.9 %all_gather.15 = s32[16,128,8]{1,2,0:T(8,128)S(1)} all-gather(s32[1,128,8]{1,2,0:T(8,128)S(1)} %copy-done.3), channel_id=1, replica_groups=mesh['pp'=2,'dp'=8,'cp'=16] {'cp'}, dimensions={0}, use_global_device_ids=true | all-gather | bytes 69632 | tf_op jit(solution)/shard_map/all_gather | solution.py:21
  79.1 0.3 reduce_window_sum.23
  79.4 25.7 %all-gather.6.cloned.1.call-done = bf16[32,128,448]{1,2,0:T(8,128)(2,1)} async-done(((bf16[2,128,448]{1,2,0:T(8,128)(2,1)}), bf16[32,128,448]{1,2,0:T(8,128)(2,1)}) %all-gather.6.cloned.1.call-update) | async-done | bytes 3670032 | tf_op jit(solution)/shard_map/all_gather | solution.py:20
  105.0 3.7 convert_bitcast_fusion
  108.7 1.7 copy.37
  110.4 4.6 %copy.38 = bf16[2560,448]{0,1:T(8,128)(2,1)} copy(bf16[2560,448]{1,0:T(8,128)(2,1)} %bitcast.46) | data formatting | bytes 4587520 | tf_op jit(solution)/shard_map/reshape | solution.py:34
  115.0 0.0 all-gather.4.cloned.1.call-update
  115.0 0.2 reduce-scatter.2.cloned.1.call-start
  115.3 0.4 select_reduce_fusion.1
  115.6 0.1 mul.45
  115.7 94.2 %all-gather.4.cloned.1.call-done = bf16[2560,3584]{0,1:T(8,128)(2,1)} async-done(((bf16[2560,448]{0,1:T(8,128)(2,1)}), bf16[2560,3584]{0,1:T(8,128)(2,1)}) %all-gather.4.cloned.1.call-update) | async-done | bytes 18350096 | tf_op jit(solution)/shard_map/all_gather | solution.py:35
  210.0 5.4 %fusion.10 = f32[1280,160]{0,1:T(8,128)S(1)} fusion(bf16[2560,3584]{0,1:T(8,128)(2,1)} %all-gather.4.cloned.1.call-done, bf16[1,1,160,3584]{3,2,1,0:T(8,128)(2,1)S(1)} %copy-done.2), kind=kOutput, calls=%fused_computation.12 | convolution fusion | flops 1468006400 | bytes 11141120 | tf_op jit(solution)/shard_map/dot_general | solution.py:43
  215.4 0.0 copy-start.6
  215.4 6.1 %fusion.12 = f32[1280,160]{0,1:T(8,128)S(1)} fusion(bf16[2560,3584]{0,1:T(8,128)(2,1)} %all-gather.4.cloned.1.call-done, bf16[1,1,160,3584]{3,2,1,0:T(8,128)(2,1)S(1)} %copy-done), kind=kOutput, calls=%fused_computation.14 | convolution fusion | flops 1468006400 | bytes 11141120 | tf_op jit(solution)/shard_map/dot_general | solution.py:42
  221.4 0.0 copy-done.5
  221.5 0.4 copy-done.6
  221.9 3.2 multiply_reduce_fusion
  225.1 8.9 %fusion.29 = f32[1280,3584]{0,1:T(8,128)} fusion(bf16[1280,160]{0,1:T(8,128)(2,1)S(1)} %get-tuple-element.9, bf16[1,1,160,3584]{3,2,1,0:T(8,128)(2,1)S(1)} %copy-done), kind=kOutput, calls=%fused_computation.27 | convolution fusion | flops 1468006400 | bytes 19906560 | tf_op jit(solution)/shard_map/dot_general | solution.py:56
  234.0 12.3 %fusion = bf16[1280,3584]{0,1:T(8,128)(2,1)} fusion(f32[1280,3584]{0,1:T(8,128)} %fusion.29, bf16[1280,160]{0,1:T(8,128)(2,1)S(1)} %get-tuple-element.10, bf16[1,1,160,3584]{3,2,1,0:T(8,128)(2,1)S(1)} %copy-done.2), kind=kOutput, calls=%fused_computation.2 | convolution fusion | flops 1477181440 | bytes 29081600 | tf_op jit(solution)/shard_map/dot_general | solution.py:58
  246.3 0.0 reduce-scatter.2.cloned.1.call-update
  246.4 0.1 copy.32
  246.5 0.2 reduce_window_sum.22
  246.7 0.7 all_to_all.12
  247.4 8.5 %all-to-all-start.1 = ((f32[16,1,80]{2,1,0:T(1,128)}), f32[16,1,80]{2,1,0:T(1,128)S(1)}, u32[]{:S(2)}, u32[]{:S(2)}) async-start(f32[16,1,80]{2,1,0:T(1,128)} %all_to_all.12), calls=%async_computation.2 | async-start | bytes 16384 | tf_op jit(solution)/shard_map/all_to_all | solution.py:73
  255.9 0.1 copy.34
  255.9 0.1 copy.33
  256.0 49.9 %reduce-scatter.2.cloned.1.call-done = bf16[1280,448]{0,1:T(8,128)(2,1)} async-done(((bf16[1280,3584]{0,1:T(8,128)(2,1)}), bf16[1280,448]{0,1:T(8,128)(2,1)}) %reduce-scatter.2.cloned.1.call-update) | async-done | bytes 1146896 | tf_op jit(solution)/shard_map/reduce_scatter | solution.py:69
  306.0 2.4 copy.39
  308.4 0.0 all-to-all-done.1
  308.4 8.5 %all-to-all-start = ((bf16[16,80,448]{2,1,0:T(8,128)(2,1)}), bf16[16,80,448]{2,1,0:T(8,128)(2,1)S(1)}, u32[]{:S(2)}, u32[]{:S(2)}) async-start(bf16[16,80,448]{2,1,0:T(8,128)(2,1)} %bitcast.9), calls=%async_computation.1 | async-start | bytes 2621440 | tf_op jit(solution)/shard_map/all_to_all | solution.py:70
  316.9 7.8 %fusion.25 = bf16[1,1,160,3584]{3,2,1,0:T(8,128)(2,1)} fusion(bf16[1280,160]{0,1:T(8,128)(2,1)S(1)} %get-tuple-element.9, bf16[2560,3584]{0,1:T(8,128)(2,1)} %all-gather.4.cloned.1.call-done), kind=kOutput, calls=%fused_computation.21 | convolution fusion | flops 1468579840 | bytes 10731520 | tf_op jit(solution)/shard_map/dot_general | solution.py:60
  324.7 7.8 %fusion.22 = bf16[1,1,160,3584]{3,2,1,0:T(8,128)(2,1)} fusion(bf16[1280,160]{0,1:T(8,128)(2,1)S(1)} %get-tuple-element.10, bf16[2560,3584]{0,1:T(8,128)(2,1)} %all-gather.4.cloned.1.call-done), kind=kOutput, calls=%fused_computation.20 | convolution fusion | flops 1468579840 | bytes 10731520 | tf_op jit(solution)/shard_map/dot_general | solution.py:63
  332.5 7.9 %fusion.21 = bf16[1,1,160,3584]{3,2,1,0:T(8,128)(2,1)} fusion(bf16[1280,160]{0,1:T(8,128)(2,1)S(1)} %copy-done.7, f32[1280]{0:T(1024)S(1)} %mul.45, bf16[2560,3584]{0,1:T(8,128)(2,1)} %all-gather.4.cloned.1.call-done), kind=kOutput, calls=%fused_computation.19 | convolution fusion | flops 1482342400 | bytes 10736640 | tf_op jit(solution)/shard_map/dot_general | solution.py:66
  340.4 12.9 %psum.7 = f32[16,80]{1,0:T(8,128)S(1)} all-reduce(f32[16,80]{1,0:T(8,128)S(1)} %bitcast.51), channel_id=1, replica_groups=mesh['pp'=2,'dp'=8,'cp'=16] {'dp'}, use_global_device_ids=true, to_apply=%region_8.9 | all-reduce | flops 1280 | bytes 10240 | tf_op jit(solution)/shard_map/psum | solution.py:76
  353.4 0.6 fusion.28
  354.0 1.3 collective-permute-start
  355.3 0.3 select_reduce_fusion
  355.6 0.6 select_reduce_fusion.2
  356.2 6.0 %collective-permute-done = bf16[128,448]{0,1:T(8,128)(2,1)S(1)} collective-permute-done((bf16[128,448]{0,1:T(8,128)(2,1)S(1)}, bf16[128,448]{0,1:T(8,128)(2,1)S(1)}, u32[]{:S(2)}, u32[]{:S(2)}) %collective-permute-start) | collective-permute-done | bytes 114720 | tf_op jit(solution)/shard_map/ppermute | solution.py:88
  362.2 0.6 copy.42
  (20 shorter events, 0.1 us)
Async XLA Ops:
  7.2 208.2 %copy-start = (bf16[1,1,160,3584]{3,2,1,0:T(8,128)(2,1)S(1)}, bf16[1,1,160,3584]{3,2,1,0:T(8,128)(2,1)}, u32[]{:S(2)}) copy-start(bf16[1,1,160,3584]{3,2,1,0:T(8,128)(2,1)} %param.11) | copy-start | bytes 3440644
  7.2 4.1 %copy-start.4 = (bf16[1,128,8]{1,2,0:T(8,128)(2,1)S(1)}, bf16[1,128,8]{1,2,0:T(8,128)(2,1)}, u32[]{:S(2)}) copy-start(bf16[1,128,8]{1,2,0:T(8,128)(2,1)} %param.9) | copy-start | bytes 6148
  7.2 37.9 %copy-start.3 = (s32[1,128,8]{1,2,0:T(8,128)S(1)}, s32[1,128,8]{1,2,0:T(8,128)}, u32[]{:S(2)}) copy-start(s32[1,128,8]{1,2,0:T(8,128)} %param.10) | copy-start | bytes 12292
  7.2 97.8 %all-gather.6.cloned.1.call-start = ((), (), s32[]{:S(2)}) async-start(), calls=%async_computation.5 | async-start | bytes 3899392 | tf_op jit(solution)/shard_map/all_gather | solution.py:20
  11.2 198.8 %all-gather.4.cloned.1.call-start = ((), (), s32[]{:S(2)}) async-start(), calls=%async_computation.3 | async-start | bytes 20643840 | tf_op jit(solution)/shard_map/all_gather | solution.py:35
  110.4 99.5 %copy-start.2 = (bf16[1,1,160,3584]{3,2,1,0:T(8,128)(2,1)S(1)}, bf16[1,1,160,3584]{3,2,1,0:T(8,128)(2,1)}, u32[]{:S(2)}) copy-start(bf16[1,1,160,3584]{3,2,1,0:T(8,128)(2,1)} %param.12) | copy-start | bytes 3440644
  115.0 190.9 %reduce-scatter.2.cloned.1.call-start = ((), (), s32[]{:S(2)}) async-start(), calls=%async_computation.4 | async-start | bytes 10321920 | tf_op jit(solution)/shard_map/reduce_scatter | solution.py:69
  209.9 11.5 %copy-start.5 = (bf16[2560,3584]{0,1:T(8,128)(2,1)S(1)}, bf16[2560,3584]{0,1:T(8,128)(2,1)}, u32[]{:S(2)}) copy-start(bf16[2560,3584]{0,1:T(8,128)(2,1)} %all-gather.4.cloned.1.call-done) | copy-start | bytes 55050244
  215.4 6.5 %copy-start.6 = (bf16[1,1,160,3584]{3,2,1,0:T(8,128)(2,1)S(1)}, bf16[1,1,160,3584]{3,2,1,0:T(8,128)(2,1)}, u32[]{:S(2)}) copy-start(bf16[1,1,160,3584]{3,2,1,0:T(8,128)(2,1)} %param.13) | copy-start | bytes 3440644
  247.4 61.0 %all-to-all-start.1 = ((f32[16,1,80]{2,1,0:T(1,128)}), f32[16,1,80]{2,1,0:T(1,128)S(1)}, u32[]{:S(2)}, u32[]{:S(2)}) async-start(f32[16,1,80]{2,1,0:T(1,128)} %all_to_all.12), calls=%async_computation.2 | async-start | bytes 16384 | tf_op jit(solution)/shard_map/all_to_all | solution.py:73
  308.4 45.0 %all-to-all-start = ((bf16[16,80,448]{2,1,0:T(8,128)(2,1)}), bf16[16,80,448]{2,1,0:T(8,128)(2,1)S(1)}, u32[]{:S(2)}, u32[]{:S(2)}) async-start(bf16[16,80,448]{2,1,0:T(8,128)(2,1)} %bitcast.9), calls=%async_computation.1 | async-start | bytes 2621440 | tf_op jit(solution)/shard_map/all_to_all | solution.py:70
  324.7 7.8 %copy-start.7 = (bf16[1280,160]{0,1:T(8,128)(2,1)S(1)}, bf16[1280,160]{0,1:T(8,128)(2,1)}, u32[]{:S(2)}) copy-start(bf16[1280,160]{0,1:T(8,128)(2,1)} %get-tuple-element.6) | copy-start | bytes 1228804
  332.5 30.3 %copy-start.1 = (bf16[1,1,160,3584]{3,2,1,0:T(8,128)(2,1)S(1)}, bf16[1,1,160,3584]{3,2,1,0:T(8,128)(2,1)}, u32[]{:S(2)}) copy-start(bf16[1,1,160,3584]{3,2,1,0:T(8,128)(2,1)} %param.11) | copy-start | bytes 3440644
  354.0 8.2 %collective-permute-start = (bf16[128,448]{0,1:T(8,128)(2,1)S(1)}, bf16[128,448]{0,1:T(8,128)(2,1)S(1)}, u32[]{:S(2)}, u32[]{:S(2)}) collective-permute-start(bf16[128,448]{0,1:T(8,128)(2,1)S(1)} %fusion.28), channel_id=1, source_target_pairs={{128,0},{129,1},{130,2},{131,3},{132,4},{133,5},{134,6},{135,7},{1... | collective-permute-start | bytes 344072 | tf_op jit(solution)/shard_map/ppermute | solution.py:88
Sparse Core Ops, SparseCore 0:
  11.3 93.6 all-gather.5
  115.1 94.7 all-gather.3
  246.5 59.4 reduce-scatter.1
where the time goes:
time: 370 us; the launch traced here: 369 us
  waiting for transfers between devices  176 us (48%)
  blocking collectives  80.7 us (22%)
  matrix products  63.8 us (17%)
  starting transfers between devices  18.6 us (5%)
  local copies, waits for them, and re-layouts  14 us (4%)
  between operations  13.9 us (4%)
    all_gather x1, waiting for transfers between devices, body(): full = lax.all_gather(rows, 'dp', axis=1, tiled=True)  94.2 us
    reduce_scatter x1, waiting for transfers between devices, body(): lax.psum_scatter(input_part, 'dp', scatter_dimension=1, tiled=True)  49.9 us
    all_gather x1, blocking collectives, body(): ids_all = lax.all_gather(expert_ids[0], 'cp')  33.9 us
    all_gather x1, blocking collectives, body(): probs_all = lax.all_gather(probs[0], 'cp')  33.8 us
    all_gather x1, waiting for transfers between devices, body(): blocks = lax.all_gather(own, 'cp')  25.7 us
    psum x1, blocking collectives, body(): back_probs = lax.psum(back_probs, 'dp')  12.9 us
    dot_general x1, matrix products, body(): jnp.dot(grad_up_pre, up_mat, preferred_element_type=jnp.float32)  12.3 us
    dot_general x1, matrix products, body(): jnp.dot(grad_gate_pre, gate_mat, preferred_element_type=jnp.float32)  8.93 us
  transfers between devices with their start and end apart: 6, of which 4 were waited for; matrix products, arithmetic and copies ran while one was open for 8% of the time, Pallas kernels for 0%

commit v1 on v0

--- a/solution.py
+++ b/solution.py
@@ -32,7 +32,9 @@
     ).astype(jnp.bfloat16)
     total_rows = experts * capacity
     rows = rows.reshape(2 * total_rows, columns)
-    full = lax.all_gather(rows, "dp", axis=1, tiled=True)
+    full = jnp.concatenate(
+        lax.all_to_all(jnp.stack([rows] * lax.axis_size("dp")), "dp", 0, 0), axis=1
+    )
     rows_in, grads_in = (full[:total_rows], full[total_rows:])
     gate_mat = w_gate[0, 0]
     up_mat = w_up[0, 0]

time: 370 us -> 484 us (1.31)
  waiting for transfers between devices: 176 us -> 281 us
  local copies, waits for them, and re-layouts: 14 us -> 29.4 us
  matrix products: 63.8 us -> 51.5 us
    all_to_all x0 -> x1, waiting for transfers between devices: none -> 201 us  [body(): lax.all_to_all(jnp.stack([rows] * lax.axis_size('dp')), 'dp', 0, 0)]
    all_gather x1 -> x0, waiting for transfers between devices: 94.2 us -> none  [body(): full = lax.all_gather(rows, 'dp', axis=1, tiled=True)]
    another operation x0 -> x2, local copies, waits for them, and re-layouts: none -> 9.61 us  [body(): jnp.stack([rows] * lax.axis_size('dp'))]
    slice x0 -> x1, local copies, waits for them, and re-layouts: none -> 7.82 us  [body(): rows_in, grads_in = (full[:total_rows], full[total_rows:])]
    all_to_all x0 -> x1, starting transfers between devices: none -> 5.86 us  [body(): lax.all_to_all(jnp.stack([rows] * lax.axis_size('dp')), 'dp', 0, 0)]
  transfers between devices with their start and end apart: 6 -> 6, of which waited for: 4 -> 4; matrix products, arithmetic and copies ran while one was open for 8% -> 5% of each run, Pallas kernels for 0% -> 0%
where the time goes in v1:
time: 484 us; the launch traced here: 483 us
  waiting for transfers between devices  281 us (58%)
  blocking collectives  81.2 us (17%)
  matrix products  51.5 us (11%)
  local copies, waits for them, and re-layouts  29.4 us (6%)
  starting transfers between devices  23.4 us (5%)
  between operations  14.3 us (3%)
    all_to_all x1, waiting for transfers between devices, body(): lax.all_to_all(jnp.stack([rows] * lax.axis_size('dp')), 'dp', 0, 0)  201 us
    reduce_scatter x1, waiting for transfers between devices, body(): lax.psum_scatter(input_part, 'dp', scatter_dimension=1, tiled=True)  48.5 us
    all_gather x1, blocking collectives, body(): ids_all = lax.all_gather(expert_ids[0], 'cp')  34.2 us
    all_gather x1, blocking collectives, body(): probs_all = lax.all_gather(probs[0], 'cp')  33.9 us
    all_gather x1, waiting for transfers between devices, body(): blocks = lax.all_gather(own, 'cp')  25.7 us
    psum x1, blocking collectives, body(): back_probs = lax.psum(back_probs, 'dp')  13.2 us
    dot_general x1, matrix products, body(): jnp.dot(grad_up_pre, up_mat, preferred_element_type=jnp.float32)  12.4 us
  transfers between devices with their start and end apart: 6, of which 4 were waited for; matrix products, arithmetic and copies ran while one was open for 5% of the time, Pallas kernels for 0%

profile of v1, /device:TPU:2, one launch (start us, length us, event | category | flops | bytes accessed | tf_op | source)
XLA Modules:
  0.0 483.3 jit_solution(610106559501658662)
XLA Ops:
  7.2 0.0 copy-start
  7.2 0.0 all-gather.3.cloned.1.call-start
  7.3 1.6 copy.36
  8.9 1.6 copy.37
  10.5 0.7 fusion.27
  11.2 0.0 all-gather.3.cloned.1.call-update
  11.2 33.9 %all_gather.13 = bf16[16,128,8]{1,2,0:T(8,128)(2,1)S(1)} all-gather(bf16[1,128,8]{1,2,0:T(8,128)(2,1)S(1)} %copy-done.6), channel_id=1, replica_groups=mesh['pp'=2,'dp'=8,'cp'=16] {'cp'}, dimensions={0}, use_global_device_ids=true | all-gather | bytes 34816 | tf_op jit(solution)/shard_map/all_gather | solution.py:22
  45.1 34.2 %all_gather.12 = s32[16,128,8]{1,2,0:T(8,128)S(1)} all-gather(s32[1,128,8]{1,2,0:T(8,128)S(1)} %copy-done.5), channel_id=1, replica_groups=mesh['pp'=2,'dp'=8,'cp'=16] {'cp'}, dimensions={0}, use_global_device_ids=true | all-gather | bytes 69632 | tf_op jit(solution)/shard_map/all_gather | solution.py:21
  79.3 0.3 reduce_window_sum.23
  79.6 25.7 %all-gather.3.cloned.1.call-done = bf16[32,128,448]{1,2,0:T(8,128)(2,1)} async-done(((bf16[2,128,448]{1,2,0:T(8,128)(2,1)}), bf16[32,128,448]{1,2,0:T(8,128)(2,1)}) %all-gather.3.cloned.1.call-update) | async-done | bytes 3670032 | tf_op jit(solution)/shard_map/all_gather | solution.py:20
  105.3 3.7 convert_bitcast_fusion
  109.0 1.7 copy.38
  110.7 3.1 copy.39
  113.9 6.5 %stack.7 = bf16[8,2560,448]{1,2,0:T(8,128)(2,1)} broadcast(bf16[2560,448]{0,1:T(8,128)(2,1)S(1)} %copy.39), dimensions={1,2} | broadcast | bytes 20643840 | tf_op jit(solution)/shard_map/stack | solution.py:36
  120.3 5.9 %all-to-all-start = ((bf16[8,2560,448]{1,2,0:T(8,128)(2,1)}), bf16[8,2560,448]{1,2,0:T(8,128)(2,1)}, u32[]{:S(2)}, u32[]{:S(2)}) async-start(bf16[8,2560,448]{1,2,0:T(8,128)(2,1)} %stack.7), calls=%async_computation | async-start | bytes 36700160 | tf_op jit(solution)/shard_map/all_to_all | solution.py:36
  126.2 0.2 reduce-scatter.2.cloned.1.call-start
  126.4 0.4 select_reduce_fusion.1
  126.8 0.1 mul.45
  126.9 200.7 %all-to-all-done = bf16[8,2560,448]{1,2,0:T(8,128)(2,1)} async-done(((bf16[8,2560,448]{1,2,0:T(8,128)(2,1)}), bf16[8,2560,448]{1,2,0:T(8,128)(2,1)}, u32[]{:S(2)}, u32[]{:S(2)}) %all-to-all-start) | async-done | bytes 18350112 | tf_op jit(solution)/shard_map/all_to_all | solution.py:36
  327.6 7.8 %fusion.29 = (bf16[1280,8,448]{0,2,1:T(8,128)(2,1)S(1)}, bf16[1280,8,448]{0,2,1:T(8,128)(2,1)S(1)}) fusion(bf16[2560,8,448]{0,2,1:T(8,128)(2,1)} %bitcast.6), kind=kLoop, calls=%fused_computation.51 | loop fusion | bytes 36700160 | tf_op jit(solution)/shard_map/slice | solution.py:38
  335.4 1.6 fusion.13
  337.1 1.9 copy-done.2
  339.0 1.6 fusion.10
  340.6 1.0 copy-done.3
  341.7 2.7 multiply_reduce_fusion
  344.3 8.9 %fusion.8 = f32[1280,3584]{0,1:T(8,128)} fusion(bf16[1280,160]{0,1:T(8,128)(2,1)S(1)} %get-tuple-element.11, bf16[1,1,160,3584]{3,2,1,0:T(8,128)(2,1)S(1)} %copy-done), kind=kOutput, calls=%fused_computation.16 | convolution fusion | flops 1468006400 | bytes 19906560 | tf_op jit(solution)/shard_map/dot_general | solution.py:58
  353.3 12.4 %fusion = bf16[1280,3584]{0,1:T(8,128)(2,1)} fusion(f32[1280,3584]{0,1:T(8,128)} %fusion.8, bf16[1280,160]{0,1:T(8,128)(2,1)S(1)} %get-tuple-element.12, bf16[1,1,160,3584]{3,2,1,0:T(8,128)(2,1)S(1)} %copy-done.4), kind=kOutput, calls=%fused_computation.2 | convolution fusion | flops 1477181440 | bytes 29081600 | tf_op jit(solution)/shard_map/dot_general | solution.py:60
  365.6 0.0 reduce-scatter.2.cloned.1.call-update
  365.7 0.7 all_to_all.16
  366.3 7.5 %all-to-all-start.2 = ((f32[16,1,80]{2,1,0:T(1,128)}), f32[16,1,80]{2,1,0:T(1,128)S(1)}, u32[]{:S(2)}, u32[]{:S(2)}) async-start(f32[16,1,80]{2,1,0:T(1,128)} %all_to_all.16), calls=%async_computation.3 | async-start | bytes 16384 | tf_op jit(solution)/shard_map/all_to_all | solution.py:75
  373.9 0.1 copy.33
  374.0 48.5 %reduce-scatter.2.cloned.1.call-done = bf16[1280,448]{0,1:T(8,128)(2,1)} async-done(((bf16[1280,3584]{0,1:T(8,128)(2,1)}), bf16[1280,448]{0,1:T(8,128)(2,1)}) %reduce-scatter.2.cloned.1.call-update) | async-done | bytes 1146896 | tf_op jit(solution)/shard_map/reduce_scatter | solution.py:71
  422.6 2.4 copy.40
  425.0 8.5 %all-to-all-start.1 = ((bf16[16,80,448]{2,1,0:T(8,128)(2,1)}), bf16[16,80,448]{2,1,0:T(8,128)(2,1)S(1)}, u32[]{:S(2)}, u32[]{:S(2)}) async-start(bf16[16,80,448]{2,1,0:T(8,128)(2,1)} %bitcast.12), calls=%async_computation.2 | async-start | bytes 2621440 | tf_op jit(solution)/shard_map/all_to_all | solution.py:72
  433.5 0.1 copy.35
  433.6 0.2 reduce_window_sum.22
  433.8 0.1 copy.34
  433.8 7.9 %fusion.5 = bf16[1,1,160,3584]{3,2,1,0:T(8,128)(2,1)} fusion(bf16[1280,160]{0,1:T(8,128)(2,1)S(1)} %get-tuple-element.11, bf16[1280,3584]{0,1:T(8,128)(2,1)} %bitcast.56), kind=kOutput, calls=%fused_computation.9 | convolution fusion | flops 1468579840 | bytes 10731520 | tf_op jit(solution)/shard_map/dot_general | solution.py:62
  441.7 7.8 %fusion.6 = bf16[1,1,160,3584]{3,2,1,0:T(8,128)(2,1)} fusion(bf16[1280,160]{0,1:T(8,128)(2,1)S(1)} %get-tuple-element.12, bf16[1280,3584]{0,1:T(8,128)(2,1)} %bitcast.57), kind=kOutput, calls=%fused_computation.10 | convolution fusion | flops 1468579840 | bytes 10731520 | tf_op jit(solution)/shard_map/dot_general | solution.py:65
  449.6 0.0 copy-start.1
  449.6 4.2 fusion.4
  453.8 13.2 %psum.7 = f32[16,80]{1,0:T(8,128)S(1)} all-reduce(f32[16,80]{1,0:T(8,128)S(1)} %bitcast.67), channel_id=1, replica_groups=mesh['pp'=2,'dp'=8,'cp'=16] {'dp'}, use_global_device_ids=true, to_apply=%region_8.9 | all-reduce | flops 1280 | bytes 10240 | tf_op jit(solution)/shard_map/psum | solution.py:78
  467.0 0.6 fusion.7
  467.7 1.3 collective-permute-start
  469.0 0.3 select_reduce_fusion
  469.3 0.6 select_reduce_fusion.2
  469.9 6.0 %collective-permute-done = bf16[128,448]{0,1:T(8,128)(2,1)S(1)} collective-permute-done((bf16[128,448]{0,1:T(8,128)(2,1)S(1)}, bf16[128,448]{0,1:T(8,128)(2,1)S(1)}, u32[]{:S(2)}, u32[]{:S(2)}) %collective-permute-start) | collective-permute-done | bytes 114720 | tf_op jit(solution)/shard_map/ppermute | solution.py:90
  475.8 0.6 copy.43
  (30 shorter events, 0.2 us)
Async XLA Ops:
  7.2 331.8 %copy-start = (bf16[1,1,160,3584]{3,2,1,0:T(8,128)(2,1)S(1)}, bf16[1,1,160,3584]{3,2,1,0:T(8,128)(2,1)}, u32[]{:S(2)}) copy-start(bf16[1,1,160,3584]{3,2,1,0:T(8,128)(2,1)} %param.11) | copy-start | bytes 3440644
  7.2 4.0 copy-start.6
  7.2 37.9 %copy-start.5 = (s32[1,128,8]{1,2,0:T(8,128)S(1)}, s32[1,128,8]{1,2,0:T(8,128)}, u32[]{:S(2)}) copy-start(s32[1,128,8]{1,2,0:T(8,128)} %param.10) | copy-start | bytes 12292
  7.2 98.1 %all-gather.3.cloned.1.call-start = ((), (), s32[]{:S(2)}) async-start(), calls=%async_computation.5 | async-start | bytes 3899392 | tf_op jit(solution)/shard_map/all_gather | solution.py:20
  120.3 207.2 %all-to-all-start = ((bf16[8,2560,448]{1,2,0:T(8,128)(2,1)}), bf16[8,2560,448]{1,2,0:T(8,128)(2,1)}, u32[]{:S(2)}, u32[]{:S(2)}) async-start(bf16[8,2560,448]{1,2,0:T(8,128)(2,1)} %stack.7), calls=%async_computation | async-start | bytes 36700160 | tf_op jit(solution)/shard_map/all_to_all | solution.py:36
  126.2 296.4 %reduce-scatter.2.cloned.1.call-start = ((), (), s32[]{:S(2)}) async-start(), calls=%async_computation.4 | async-start | bytes 10321920 | tf_op jit(solution)/shard_map/reduce_scatter | solution.py:71
  327.5 7.9 %copy-start.4 = (bf16[1,1,160,3584]{3,2,1,0:T(8,128)(2,1)S(1)}, bf16[1,1,160,3584]{3,2,1,0:T(8,128)(2,1)}, u32[]{:S(2)}) copy-start(bf16[1,1,160,3584]{3,2,1,0:T(8,128)(2,1)} %param.12) | copy-start | bytes 3440644
  335.4 3.6 copy-start.2
  335.4 6.3 %copy-start.3 = (bf16[1280,8,448]{0,2,1:T(8,128)(2,1)}, bf16[1280,8,448]{0,2,1:T(8,128)(2,1)S(1)}, u32[]{:S(2)}) copy-start(bf16[1280,8,448]{0,2,1:T(8,128)(2,1)S(1)} %get-tuple-element.9) | copy-start | bytes 27525124
  339.0 2.7 copy-start.7
  366.3 58.6 %all-to-all-start.2 = ((f32[16,1,80]{2,1,0:T(1,128)}), f32[16,1,80]{2,1,0:T(1,128)S(1)}, u32[]{:S(2)}, u32[]{:S(2)}) async-start(f32[16,1,80]{2,1,0:T(1,128)} %all_to_all.16), calls=%async_computation.3 | async-start | bytes 16384 | tf_op jit(solution)/shard_map/all_to_all | solution.py:75
  425.0 42.0 %all-to-all-start.1 = ((bf16[16,80,448]{2,1,0:T(8,128)(2,1)}), bf16[16,80,448]{2,1,0:T(8,128)(2,1)S(1)}, u32[]{:S(2)}, u32[]{:S(2)}) async-start(bf16[16,80,448]{2,1,0:T(8,128)(2,1)} %bitcast.12), calls=%async_computation.2 | async-start | bytes 2621440 | tf_op jit(solution)/shard_map/all_to_all | solution.py:72
  433.8 15.7 %slice-start = ((s8[9175040]{0:T(1024)(128)(4,1)}), s8[4194304]{0:T(1024)(128)(4,1)S(1)}, s32[]{:S(2)}) async-start(s8[9175040]{0:T(1024)(128)(4,1)} %bitcast.60), calls=%async_computation.6 | async-start | bytes 8388608
  433.8 15.7 %slice-start.1 = ((s8[9175040]{0:T(1024)(128)(4,1)}), s8[4194304]{0:T(1024)(128)(4,1)S(1)}, s32[]{:S(2)}) async-start(s8[9175040]{0:T(1024)(128)(4,1)} %bitcast.60), calls=%async_computation.7 | async-start | bytes 8388608
  441.7 7.8 %slice-start.2 = ((s8[9175040]{0:T(1024)(128)(4,1)}), s8[786432]{0:T(1024)(128)(4,1)S(1)}, s32[]{:S(2)}) async-start(s8[9175040]{0:T(1024)(128)(4,1)} %bitcast.60), calls=%async_computation.8 | async-start | bytes 1572864
  441.7 7.8 %copy-start.8 = (bf16[1280,160]{0,1:T(8,128)(2,1)S(1)}, bf16[1280,160]{0,1:T(8,128)(2,1)}, u32[]{:S(2)}) copy-start(bf16[1280,160]{0,1:T(8,128)(2,1)} %get-tuple-element.6) | copy-start | bytes 1228804
  449.6 26.9 %copy-start.1 = (bf16[1,1,160,3584]{3,2,1,0:T(8,128)(2,1)S(1)}, bf16[1,1,160,3584]{3,2,1,0:T(8,128)(2,1)}, u32[]{:S(2)}) copy-start(bf16[1,1,160,3584]{3,2,1,0:T(8,128)(2,1)} %param.11) | copy-start | bytes 3440644
  467.7 8.2 %collective-permute-start = (bf16[128,448]{0,1:T(8,128)(2,1)S(1)}, bf16[128,448]{0,1:T(8,128)(2,1)S(1)}, u32[]{:S(2)}, u32[]{:S(2)}) collective-permute-start(bf16[128,448]{0,1:T(8,128)(2,1)S(1)} %fusion.7), channel_id=1, source_target_pairs={{128,0},{129,1},{130,2},{131,3},{132,4},{133,5},{134,6},{135,7},{1... | collective-permute-start | bytes 344072 | tf_op jit(solution)/shard_map/ppermute | solution.py:90
Sparse Core Ops, SparseCore 0:
  11.3 93.9 all-gather.2
  365.8 56.7 reduce-scatter.1
